TPU v7x, 32 devices: a whole 2x2x4 slice. The times are simulated.
32 devices in a mesh: dp: 2 (over core), blk: 4 (over y, x), rep: 4 (over z).
Axes of the slice: x: 2, y: 2, z: 4, core: 2. Of those that a mesh axis runs over, the one named last changes fastest.
Arguments:
- feats: bfloat16 [2, 16384, 512], P('dp', ('blk', 'rep')), may hold values from -6 to 6
- weight: bfloat16 [512, 512], replicated, may hold values from -0.25 to 0.25
- cols: int32 [2, 128, 15], P('dp', ('blk', 'rep')), may hold values from -1 to 127, as said below
- vals: bfloat16 [2, 128, 15, 128, 128], P('dp', ('blk', 'rep')), as said below
- cotangent: bfloat16 [2, 16384, 512], P('dp', ('blk', 'rep')), may hold values from -6 to 6
Outputs:
- activ: bfloat16 [2, 16384, 512], P('dp', ('blk', 'rep'))
- feat_grad: bfloat16 [2, 16384, 512], P('dp', ('blk', 'rep'))
- weight_grad: float32 [512, 512], replicated
Inputs may be any that keep to these rules, and one draw needn't show every extreme that they name: `cols`: used slots come first in each row and -1 marks the unused ones. Slot 0 of block row p names p itself; every other used slot names a block at most 7 away from p, each at most once. The relation is symmetric: p names q exactly when q names p. In every scenario some block row uses all 15 slots. `vals`: the block in row p's slot naming q is the transpose of the block in row q's slot naming p (the self block is symmetric); unused slots hold zeros.
All inputs are finite; a program needn't handle non-finite values.
Results may differ from a plain program's by a relative error of at most 0.0061.
Values may be sent and summed in bfloat16 or wider, within the bound.
No kernel may reach another device: no remote copies, remote signals or barrier semaphores. Data moves between devices by JAX's collectives and lax.ppermute only.
A program may use at most 128 MiB of HBM per device.

v0:
```python
import jax
import jax.numpy as jnp
from jax import lax
from jax.sharding import PartitionSpec as P

REACH = 7


def padded(cells, sides, width):
    for axis, dim in sides:
        count = lax.axis_size(axis)
        ends = count - 1
        head = lax.slice_in_dim(cells, 0, width, axis=dim)
        tail = lax.slice_in_dim(cells, cells.shape[dim] - width, cells.shape[dim], axis=dim)
        cells = jnp.concatenate(
            [
                lax.ppermute(tail, axis, [(i, (i + 1) % count) for i in range(ends)]),
                cells,
                lax.ppermute(head, axis, [((i + 1) % count, i) for i in range(ends)]),
            ],
            axis=dim,
        )
    return cells


def spread(extended, row_cols, row_vals, first):
    row_blocks = row_vals.shape[0]
    block_size = row_vals.shape[2]
    width = extended.shape[1]
    ext_blocks = extended.reshape(-1, block_size, width)
    margin = (ext_blocks.shape[0] - row_blocks) // 2
    local_index = jnp.where(row_cols >= 0, row_cols - first + margin, 0)
    picked = ext_blocks[local_index]
    summed = jnp.einsum("rkab,rkbf->raf", row_vals, picked, preferred_element_type=jnp.float32)
    return summed.reshape(-1, width)


def shards(feats, weight, cols, vals, cotangent):
    first = lax.axis_index(("blk", "rep")) * cols.shape[1]
    rim_rows = REACH * vals.shape[3]
    own = feats[0]
    projected = jnp.dot(own, weight, preferred_element_type=jnp.float32).astype(jnp.bfloat16)
    extended = padded(projected, ((("blk", "rep"), 0),), rim_rows)
    agg = spread(extended, cols[0], vals[0], first)
    sig = jax.nn.sigmoid(agg)
    activ_list = [(agg * sig).astype(jnp.bfloat16)]
    dagg = (cotangent[0].astype(jnp.float32) * sig * (1.0 + agg * (1.0 - sig))).astype(jnp.bfloat16)
    grad_ext = padded(dagg, ((("blk", "rep"), 0),), rim_rows)
    dproj = spread(grad_ext, cols[0], vals[0], first).astype(jnp.bfloat16)
    back = lax.dot_general(
        dproj, weight, (((1,), (1,)), ((), ())), preferred_element_type=jnp.float32
    )
    grad_list = [back.astype(jnp.bfloat16)]
    grads = lax.dot_general(
        own, dproj, (((0,), (0,)), ((), ())), preferred_element_type=jnp.float32
    )
    weight_grad = lax.psum(grads, ("dp", "blk", "rep"))
    return (jnp.stack(activ_list), jnp.stack(grad_list), weight_grad)


def solution(mesh):
    placed = (
        P("dp", ("blk", "rep"), None),
        P(),
        P("dp", ("blk", "rep"), None),
        P("dp", ("blk", "rep"), None, None, None),
        P("dp", ("blk", "rep"), None),
    )
    return jax.shard_map(
        shards,
        mesh=mesh,
        in_specs=placed,
        out_specs=(P("dp", ("blk", "rep"), None), P("dp", ("blk", "rep"), None), P()),
        check_vma=False,
    )
```

profile of v0, /device:TPU:0, one launch (start us, length us, event | category | flops | bytes accessed | tf_op | source)
XLA Modules:
  0.0 287.8 jit_solution(11901660477694064899)
XLA Ops:
  7.2 1.2 copy-done
  8.4 1.7 convolution_convert_fusion.1
  10.1 1.1 fusion.16
  11.2 5.9 %collective-permute-start = (bf16[896,512]{1,0:T(8,128)(2,1)}, bf16[896,512]{1,0:T(8,128)(2,1)}, u32[]{:S(2)}, u32[]{:S(2)}) collective-permute-start(bf16[896,512]{1,0:T(8,128)(2,1)} %get-tuple-element.8), channel_id=1, source_target_pairs={{0,1},{1,2},{2,3},{3,4},{4,5},{5,6},{6,7},{7,8},{8,9},{9,10},{10,1... | collective-permute-start | bytes 2752520 | tf_op jit(solution)/shard_map/ppermute | solution.py:17
  17.1 1.3 collective-permute-start.1
  18.5 17.5 %collective-permute-done = bf16[896,512]{1,0:T(8,128)(2,1)} collective-permute-done((bf16[896,512]{1,0:T(8,128)(2,1)}, bf16[896,512]{1,0:T(8,128)(2,1)}, u32[]{:S(2)}, u32[]{:S(2)}) %collective-permute-start) | collective-permute-done | bytes 917536 | tf_op jit(solution)/shard_map/ppermute | solution.py:17
  36.1 23.3 %collective-permute-done.1 = bf16[896,512]{1,0:T(8,128)(2,1)} collective-permute-done((bf16[896,512]{1,0:T(8,128)(2,1)S(1)}, bf16[896,512]{1,0:T(8,128)(2,1)}, u32[]{:S(2)}, u32[]{:S(2)}) %collective-permute-start.1) | collective-permute-done | bytes 917536 | tf_op jit(solution)/shard_map/ppermute | solution.py:19
  59.3 3.2 %pad_maximum_fusion = bf16[2816,512]{1,0:T(8,128)(2,1)} fusion(bf16[896,512]{1,0:T(8,128)(2,1)} %collective-permute-done.1, bf16[1024,512]{1,0:T(8,128)(2,1)S(1)} %convolution_convert_fusion.1, bf16[896,512]{1,0:T(8,128)(2,1)} %collective-permute-done), kind=kLoop, calls=%fused_computation.6 | loop fusion | flops 8650752 | bytes 5767168 | tf_op jit(solution)/shard_map/concatenate | solution.py:15
  62.6 9.5 %gather_fusion = bf16[120,128,512]{2,1,0:T(8,128)(2,1)} fusion(bf16[22,128,512]{2,1,0:T(8,128)(2,1)} %bitcast.62, s32[1024]{0:T(1024)S(1)} %pad_clamp_fusion), kind=kCustom, calls=%fused_computation | custom fusion | bytes 31457760 | tf_op jit(solution)/shard_map/gather | solution.py:33
  72.1 8.2 %fusion = f32[8,512,128,1]{1,2,3,0:T(8,128)S(1)} fusion(bf16[8,15,128,512]{3,2,1,0:T(8,128)(2,1)} %bitcast.64, bf16[1,8,15,128,128]{4,3,2,1,0:T(8,128)(2,1)} %param.8), kind=kOutput, calls=%fused_computation.2 | convolution fusion | flops 2013265920 | bytes 21757952 | tf_op jit(solution)/shard_map/rkab,rkbf->raf/dot_general | solution.py:34
  80.3 0.8 fusion.5
  81.3 2.5 collective-permute-start.2
  83.8 1.3 collective-permute-start.3
  85.1 18.4 %collective-permute-done.2 = bf16[896,512]{1,0:T(8,128)(2,1)S(1)} collective-permute-done((bf16[896,512]{1,0:T(8,128)(2,1)S(1)}, bf16[896,512]{1,0:T(8,128)(2,1)S(1)}, u32[]{:S(2)}, u32[]{:S(2)}) %collective-permute-start.2) | collective-permute-done | bytes 917536 | tf_op jit(solution)/shard_map/ppermute | solution.py:17
  103.5 23.8 %collective-permute-done.3 = bf16[896,512]{1,0:T(8,128)(2,1)S(1)} collective-permute-done((bf16[896,512]{1,0:T(8,128)(2,1)S(1)}, bf16[896,512]{1,0:T(8,128)(2,1)S(1)}, u32[]{:S(2)}, u32[]{:S(2)}) %collective-permute-start.3) | collective-permute-done | bytes 917536 | tf_op jit(solution)/shard_map/ppermute | solution.py:19
  127.3 1.8 pad_maximum_fusion.1
  129.1 9.5 %gather_fusion.1 = bf16[120,128,512]{2,1,0:T(8,128)(2,1)} fusion(bf16[22,128,512]{2,1,0:T(8,128)(2,1)} %bitcast.61, s32[1024]{0:T(1024)S(1)} %pad_clamp_fusion), kind=kCustom, calls=%fused_computation.1 | custom fusion | bytes 31457760 | tf_op jit(solution)/shard_map/gather | solution.py:33
  138.6 9.0 %bitcast_convert_fusion = bf16[8,512,128]{1,2,0:T(8,128)(2,1)S(1)} fusion(bf16[8,15,128,512]{3,2,1,0:T(8,128)(2,1)} %bitcast.63, bf16[1,8,15,128,128]{4,3,2,1,0:T(8,128)(2,1)} %param.8), kind=kOutput, calls=%fused_computation.11 | convolution fusion | flops 2013790208 | bytes 20709376 | tf_op jit(solution)/shard_map/rkab,rkbf->raf/dot_general | solution.py:34
  147.7 1.0 copy-done.1
  148.6 1.7 convolution_bitcast_fusion
  150.4 1.5 multiply_convert_fusion
  151.9 1.7 fusion.12
  153.6 124.8 %all-reduce.2.cloned.1.call-done = f32[512,512]{0,1:T(8,128)} async-done(((f32[512,512]{0,1:T(8,128)}), f32[512,512]{0,1:T(8,128)}) %all-reduce.2.cloned.1.call-update) | async-done | bytes 1048592 | tf_op jit(solution)/shard_map/psum | solution.py:57
  278.4 2.5 copy.8
  (16 shorter events, 0.3 us)
Async XLA Ops:
  7.2 1.2 copy-start
  7.2 11.2 %copy-start.4 = (s32[1,8,15]{2,1,0:T(8,128)S(1)}, s32[1,8,15]{2,1,0:T(8,128)}, u32[]{:S(2)}) copy-start(s32[1,8,15]{2,1,0:T(8,128)} %param.7) | copy-start | bytes 1444
  7.2 271.2 %all-reduce.2.cloned.1.call-start = ((), (), s32[]{:S(2)}) async-start(), calls=%async_computation | async-start | bytes 2097152 | tf_op jit(solution)/shard_map/psum | solution.py:57
  11.2 24.8 %collective-permute-start = (bf16[896,512]{1,0:T(8,128)(2,1)}, bf16[896,512]{1,0:T(8,128)(2,1)}, u32[]{:S(2)}, u32[]{:S(2)}) collective-permute-start(bf16[896,512]{1,0:T(8,128)(2,1)} %get-tuple-element.8), channel_id=1, source_target_pairs={{0,1},{1,2},{2,3},{3,4},{4,5},{5,6},{6,7},{7,8},{8,9},{9,10},{10,1... | collective-permute-start | bytes 2752520 | tf_op jit(solution)/shard_map/ppermute | solution.py:17
  17.1 42.2 %collective-permute-start.1 = (bf16[896,512]{1,0:T(8,128)(2,1)S(1)}, bf16[896,512]{1,0:T(8,128)(2,1)}, u32[]{:S(2)}, u32[]{:S(2)}) collective-permute-start(bf16[896,512]{1,0:T(8,128)(2,1)S(1)} %get-tuple-element.9), channel_id=1, source_target_pairs={{1,0},{2,1},{3,2},{4,3},{5,4},{6,5},{7,6},{8,7},{9,8},{10,9},{11,1... | collective-permute-start | bytes 2752520 | tf_op jit(solution)/shard_map/ppermute | solution.py:19
  72.1 8.2 %copy-start.3 = (bf16[1,1024,512]{2,1,0:T(8,128)(2,1)S(1)}, bf16[1,1024,512]{2,1,0:T(8,128)(2,1)}, u32[]{:S(2)}) copy-start(bf16[1,1024,512]{2,1,0:T(8,128)(2,1)} %param.9) | copy-start | bytes 3145732
  81.3 22.2 %collective-permute-start.2 = (bf16[896,512]{1,0:T(8,128)(2,1)S(1)}, bf16[896,512]{1,0:T(8,128)(2,1)S(1)}, u32[]{:S(2)}, u32[]{:S(2)}) collective-permute-start(bf16[896,512]{1,0:T(8,128)(2,1)S(1)} %get-tuple-element.6), channel_id=1, source_target_pairs={{0,1},{1,2},{2,3},{3,4},{4,5},{5,6},{6,7},{7,8},{8,9},{9,10},{10,1... | collective-permute-start | bytes 2752520 | tf_op jit(solution)/shard_map/ppermute | solution.py:17
  83.8 43.5 %collective-permute-start.3 = (bf16[896,512]{1,0:T(8,128)(2,1)S(1)}, bf16[896,512]{1,0:T(8,128)(2,1)S(1)}, u32[]{:S(2)}, u32[]{:S(2)}) collective-permute-start(bf16[896,512]{1,0:T(8,128)(2,1)S(1)} %get-tuple-element.7), channel_id=1, source_target_pairs={{1,0},{2,1},{3,2},{4,3},{5,4},{6,5},{7,6},{8,7},{9,8},{10,9},{11,1... | collective-permute-start | bytes 2752520 | tf_op jit(solution)/shard_map/ppermute | solution.py:19
  147.6 1.0 copy-start.1
  150.4 1.5 copy-start.2
  150.4 1.5 copy-start.5
Sparse Core Ops, SparseCore 0:
  150.5 127.8 all-reduce.1
where the time goes:
time: 288 us
  waiting for transfers between devices  208 us (72%)
  local copies, waits for them, and re-layouts  25 us (9%)
  matrix products  22.4 us (8%)
  between operations  14.2 us (5%)
  starting transfers between devices  11 us (4%)
  other arithmetic  7.32 us (3%)
    psum x1, waiting for transfers between devices, shards(): weight_grad = lax.psum(grads, ('dp', 'blk', 'rep'))  125 us
    ppermute x2, waiting for transfers between devices, padded(): lax.ppermute(head, axis, [((i + 1) % count, i) for i in range(ends)])  47.1 us
    ppermute x2, waiting for transfers between devices, padded(): lax.ppermute(tail, axis, [(i, (i + 1) % count) for i in range(ends)])  35.9 us
    gather x2, local copies, waits for them, and re-layouts, spread(): picked = ext_blocks[local_index]  19 us
    dot_general x2, matrix products, spread(): jnp.einsum('rkab,rkbf->raf', row_vals, picked, preferred_element_type=jnp...  17.2 us
    ppermute x2, starting transfers between devices, padded(): lax.ppermute(tail, axis, [(i, (i + 1) % count) for i in range(ends)])  8.42 us
  transfers between devices with their start and end apart: 5, of which 5 were waited for; matrix products, arithmetic and copies ran while one was open for 1% of the time, Pallas kernels for 0%

commit v1 on v0

--- a/solution.py
+++ b/solution.py
@@ -54,7 +54,7 @@
     grads = lax.dot_general(
         own, dproj, (((0,), (0,)), ((), ())), preferred_element_type=jnp.float32
     )
-    weight_grad = lax.psum(grads, ("dp", "blk", "rep"))
+    weight_grad = lax.psum(lax.psum(grads, ("blk", "rep")), "dp")
     return (jnp.stack(activ_list), jnp.stack(grad_list), weight_grad)
 
 

time: 288 us -> 291 us (1.010)
  waiting for transfers between devices: 208 us -> 211 us
    psum x1 -> x2, waiting for transfers between devices: 125 us -> 128 us  [shards(): weight_grad = lax.psum(lax.psum(grads, ('blk', 'rep')), 'dp')]
  transfers between devices with their start and end apart: 5 -> 6, of which waited for: 5 -> 6; matrix products, arithmetic and copies ran while one was open for 1% -> 1% of each run, Pallas kernels for 0% -> 0%
where the time goes in v1:
time: 291 us
  waiting for transfers between devices  211 us (73%)
  local copies, waits for them, and re-layouts  25 us (9%)
  matrix products  22.4 us (8%)
  between operations  14.2 us (5%)
  starting transfers between devices  11.1 us (4%)
  other arithmetic  7.32 us (3%)
    psum x2, waiting for transfers between devices, shards(): weight_grad = lax.psum(lax.psum(grads, ('blk', 'rep')), 'dp')  128 us
    ppermute x2, waiting for transfers between devices, padded(): lax.ppermute(head, axis, [((i + 1) % count, i) for i in range(ends)])  47.1 us
    ppermute x2, waiting for transfers between devices, padded(): lax.ppermute(tail, axis, [(i, (i + 1) % count) for i in range(ends)])  35.9 us
    gather x2, local copies, waits for them, and re-layouts, spread(): picked = ext_blocks[local_index]  19 us
    dot_general x2, matrix products, spread(): jnp.einsum('rkab,rkbf->raf', row_vals, picked, preferred_element_type=jnp...  17.2 us
    ppermute x2, starting transfers between devices, padded(): lax.ppermute(tail, axis, [(i, (i + 1) % count) for i in range(ends)])  8.42 us
  transfers between devices with their start and end apart: 6, of which 6 were waited for; matrix products, arithmetic and copies ran while one was open for 1% of the time, Pallas kernels for 0%

profile of v1, /device:TPU:0, one launch (start us, length us, event | category | flops | bytes accessed | tf_op | source)
XLA Modules:
  0.0 290.7 jit_solution(3680276255962899780)
XLA Ops:
  7.2 1.2 copy-done
  8.4 1.7 convolution_convert_fusion.1
  10.1 1.1 fusion.16
  11.2 5.9 %collective-permute-start = (bf16[896,512]{1,0:T(8,128)(2,1)}, bf16[896,512]{1,0:T(8,128)(2,1)}, u32[]{:S(2)}, u32[]{:S(2)}) collective-permute-start(bf16[896,512]{1,0:T(8,128)(2,1)} %get-tuple-element.8), channel_id=1, source_target_pairs={{0,1},{1,2},{2,3},{3,4},{4,5},{5,6},{6,7},{7,8},{8,9},{9,10},{10,1... | collective-permute-start | bytes 2752520 | tf_op jit(solution)/shard_map/ppermute | solution.py:17
  17.1 1.3 collective-permute-start.1
  18.5 17.5 %collective-permute-done = bf16[896,512]{1,0:T(8,128)(2,1)} collective-permute-done((bf16[896,512]{1,0:T(8,128)(2,1)}, bf16[896,512]{1,0:T(8,128)(2,1)}, u32[]{:S(2)}, u32[]{:S(2)}) %collective-permute-start) | collective-permute-done | bytes 917536 | tf_op jit(solution)/shard_map/ppermute | solution.py:17
  36.1 23.3 %collective-permute-done.1 = bf16[896,512]{1,0:T(8,128)(2,1)} collective-permute-done((bf16[896,512]{1,0:T(8,128)(2,1)S(1)}, bf16[896,512]{1,0:T(8,128)(2,1)}, u32[]{:S(2)}, u32[]{:S(2)}) %collective-permute-start.1) | collective-permute-done | bytes 917536 | tf_op jit(solution)/shard_map/ppermute | solution.py:19
  59.3 3.2 %pad_maximum_fusion = bf16[2816,512]{1,0:T(8,128)(2,1)} fusion(bf16[896,512]{1,0:T(8,128)(2,1)} %collective-permute-done.1, bf16[1024,512]{1,0:T(8,128)(2,1)S(1)} %convolution_convert_fusion.1, bf16[896,512]{1,0:T(8,128)(2,1)} %collective-permute-done), kind=kLoop, calls=%fused_computation.6 | loop fusion | flops 8650752 | bytes 5767168 | tf_op jit(solution)/shard_map/concatenate | solution.py:15
  62.6 9.5 %gather_fusion = bf16[120,128,512]{2,1,0:T(8,128)(2,1)} fusion(bf16[22,128,512]{2,1,0:T(8,128)(2,1)} %bitcast.62, s32[1024]{0:T(1024)S(1)} %pad_clamp_fusion), kind=kCustom, calls=%fused_computation | custom fusion | bytes 31457760 | tf_op jit(solution)/shard_map/gather | solution.py:33
  72.1 8.2 %fusion = f32[8,512,128,1]{1,2,3,0:T(8,128)S(1)} fusion(bf16[8,15,128,512]{3,2,1,0:T(8,128)(2,1)} %bitcast.64, bf16[1,8,15,128,128]{4,3,2,1,0:T(8,128)(2,1)} %param.8), kind=kOutput, calls=%fused_computation.2 | convolution fusion | flops 2013265920 | bytes 21757952 | tf_op jit(solution)/shard_map/rkab,rkbf->raf/dot_general | solution.py:34
  81.3 2.5 collective-permute-start.2
  83.8 1.3 collective-permute-start.3
  85.1 18.4 %collective-permute-done.2 = bf16[896,512]{1,0:T(8,128)(2,1)S(1)} collective-permute-done((bf16[896,512]{1,0:T(8,128)(2,1)S(1)}, bf16[896,512]{1,0:T(8,128)(2,1)S(1)}, u32[]{:S(2)}, u32[]{:S(2)}) %collective-permute-start.2) | collective-permute-done | bytes 917536 | tf_op jit(solution)/shard_map/ppermute | solution.py:17
  103.5 23.8 %collective-permute-done.3 = bf16[896,512]{1,0:T(8,128)(2,1)S(1)} collective-permute-done((bf16[896,512]{1,0:T(8,128)(2,1)S(1)}, bf16[896,512]{1,0:T(8,128)(2,1)S(1)}, u32[]{:S(2)}, u32[]{:S(2)}) %collective-permute-start.3) | collective-permute-done | bytes 917536 | tf_op jit(solution)/shard_map/ppermute | solution.py:19
  127.3 1.8 pad_maximum_fusion.1
  129.1 9.5 %gather_fusion.1 = bf16[120,128,512]{2,1,0:T(8,128)(2,1)} fusion(bf16[22,128,512]{2,1,0:T(8,128)(2,1)} %bitcast.61, s32[1024]{0:T(1024)S(1)} %pad_clamp_fusion), kind=kCustom, calls=%fused_computation.1 | custom fusion | bytes 31457760 | tf_op jit(solution)/shard_map/gather | solution.py:33
  138.6 9.0 %bitcast_convert_fusion = bf16[8,512,128]{1,2,0:T(8,128)(2,1)S(1)} fusion(bf16[8,15,128,512]{3,2,1,0:T(8,128)(2,1)} %bitcast.63, bf16[1,8,15,128,128]{4,3,2,1,0:T(8,128)(2,1)} %param.8), kind=kOutput, calls=%fused_computation.11 | convolution fusion | flops 2013790208 | bytes 20709376 | tf_op jit(solution)/shard_map/rkab,rkbf->raf/dot_general | solution.py:34
  147.7 1.0 copy-done.1
  148.6 1.7 convolution_bitcast_fusion
  150.4 109.9 %all-reduce.3.cloned.1.call-done = f32[512,512]{0,1:T(8,128)} async-done(((f32[512,512]{0,1:T(8,128)}), f32[512,512]{0,1:T(8,128)}) %all-reduce.3.cloned.1.call-update) | async-done | bytes 1048592 | tf_op jit(solution)/shard_map/psum | solution.py:57
  260.4 1.5 multiply_convert_fusion
  261.9 1.7 fusion.12
  263.6 17.8 %all-reduce.5.cloned.1.call-done = f32[512,512]{0,1:T(8,128)} async-done(((f32[512,512]{0,1:T(8,128)}), f32[512,512]{0,1:T(8,128)}) %all-reduce.5.cloned.1.call-update) | async-done | bytes 1048592 | tf_op jit(solution)/shard_map/psum | solution.py:57
  281.4 2.5 copy.8
  (19 shorter events, 1.2 us)
Async XLA Ops:
  7.2 1.2 copy-start
  7.2 11.2 %copy-start.4 = (s32[1,8,15]{2,1,0:T(8,128)S(1)}, s32[1,8,15]{2,1,0:T(8,128)}, u32[]{:S(2)}) copy-start(s32[1,8,15]{2,1,0:T(8,128)} %param.7) | copy-start | bytes 1444
  7.2 253.1 %all-reduce.3.cloned.1.call-start = ((), (), s32[]{:S(2)}) async-start(), calls=%async_computation | async-start | bytes 2097152 | tf_op jit(solution)/shard_map/psum | solution.py:57
  11.2 24.8 %collective-permute-start = (bf16[896,512]{1,0:T(8,128)(2,1)}, bf16[896,512]{1,0:T(8,128)(2,1)}, u32[]{:S(2)}, u32[]{:S(2)}) collective-permute-start(bf16[896,512]{1,0:T(8,128)(2,1)} %get-tuple-element.8), channel_id=1, source_target_pairs={{0,1},{1,2},{2,3},{3,4},{4,5},{5,6},{6,7},{7,8},{8,9},{9,10},{10,1... | collective-permute-start | bytes 2752520 | tf_op jit(solution)/shard_map/ppermute | solution.py:17
  17.1 42.2 %collective-permute-start.1 = (bf16[896,512]{1,0:T(8,128)(2,1)S(1)}, bf16[896,512]{1,0:T(8,128)(2,1)}, u32[]{:S(2)}, u32[]{:S(2)}) collective-permute-start(bf16[896,512]{1,0:T(8,128)(2,1)S(1)} %get-tuple-element.9), channel_id=1, source_target_pairs={{1,0},{2,1},{3,2},{4,3},{5,4},{6,5},{7,6},{8,7},{9,8},{10,9},{11,1... | collective-permute-start | bytes 2752520 | tf_op jit(solution)/shard_map/ppermute | solution.py:19
  72.1 8.2 %copy-start.3 = (bf16[1,1024,512]{2,1,0:T(8,128)(2,1)S(1)}, bf16[1,1024,512]{2,1,0:T(8,128)(2,1)}, u32[]{:S(2)}) copy-start(bf16[1,1024,512]{2,1,0:T(8,128)(2,1)} %param.9) | copy-start | bytes 3145732
  81.3 22.2 %collective-permute-start.2 = (bf16[896,512]{1,0:T(8,128)(2,1)S(1)}, bf16[896,512]{1,0:T(8,128)(2,1)S(1)}, u32[]{:S(2)}, u32[]{:S(2)}) collective-permute-start(bf16[896,512]{1,0:T(8,128)(2,1)S(1)} %get-tuple-element.6), channel_id=1, source_target_pairs={{0,1},{1,2},{2,3},{3,4},{4,5},{5,6},{6,7},{7,8},{8,9},{9,10},{10,1... | collective-permute-start | bytes 2752520 | tf_op jit(solution)/shard_map/ppermute | solution.py:17
  83.8 43.5 %collective-permute-start.3 = (bf16[896,512]{1,0:T(8,128)(2,1)S(1)}, bf16[896,512]{1,0:T(8,128)(2,1)S(1)}, u32[]{:S(2)}, u32[]{:S(2)}) collective-permute-start(bf16[896,512]{1,0:T(8,128)(2,1)S(1)} %get-tuple-element.7), channel_id=1, source_target_pairs={{1,0},{2,1},{3,2},{4,3},{5,4},{6,5},{7,6},{8,7},{9,8},{10,9},{11,1... | collective-permute-start | bytes 2752520 | tf_op jit(solution)/shard_map/ppermute | solution.py:19
  147.6 1.0 copy-start.1
  150.3 131.0 %all-reduce.5.cloned.1.call-start = ((), (), s32[]{:S(2)}) async-start(), calls=%async_computation.1 | async-start | bytes 2097152 | tf_op jit(solution)/shard_map/psum | solution.py:57
  260.3 1.5 copy-start.2
  260.4 1.5 copy-start.5
Sparse Core Ops, SparseCore 0:
  150.5 109.8 all-reduce.2
  262.7 18.6 all-reduce.4
